TPU v7x, 32 devices: a whole 2x2x4 slice. The times are simulated.
32 devices in a mesh: groups: 2 (over y), resp: 4 (over z), section: 4 (over x, core).
Axes of the slice: x: 2, y: 2, z: 4, core: 2. Of those that a mesh axis runs over, the one named last changes fastest.
Arguments:
- completion_rows: bfloat16 [2, 8, 64, 4096], P(None, ('groups', 'resp')), parts along dimension 1, may hold values from -16 to 16
- prompt_pool: bfloat16 [4, 8, 64, 4096], P('section', ('groups', 'resp')), parts along dimension 1, may hold values from -16 to 16
- norm_gain: float32 [4, 4096], P('section'), may hold values from 0.5 to 1.5
- short_taps: float32 [4, 7, 4096], P('section'), may hold values from -2.4 to 2.4
- long_taps: float32 [4, 128, 256], P('section'), may hold values from -0.5 to 0.5
- score_head: float32 [4096], replicated, may hold values from -0.09375 to 0.09375
- live_lengths: int32 [2, 8], P(None, ('groups', 'resp')), parts along dimension 1, may hold values from 16 to 64, as said below
- prompt_owner: int32 [4], P('groups'), parts along dimension 0, may hold values from 0 to 3
- pair_index: int32 [2, 16, 2], P(None, 'groups'), parts along dimension 1, may hold values from 0 to 3
Outputs:
- scores: bfloat16 [2, 8], P(None, ('groups', 'resp')), parts along dimension 1
- gain_grad: float32 [4, 8192], P('section', 'groups'), parts along dimension 1
- short_grad: float32 [4, 14, 4096], P('section', 'groups'), parts along dimension 1
- long_grad: float32 [4, 256, 256], P('section', 'groups'), parts along dimension 1
There are 2 independent parts, one for each index of `groups`. A program takes and returns all parts, laid end to end along the dimension named above; an argument that names none is the same for every part. Nothing has to cross between parts.
Inputs may be any that keep to these rules, and one draw needn't show every extreme that they name: `live_lengths`: live rows of each completion, counted from its first row; in each microbatch one completion has all 64 rows live and another a quarter of 64. `pair_index`: the two members of a pair may coincide.
All inputs are finite; a program needn't handle non-finite values.
Results may differ from a plain program's by a relative error of at most 0.0097.
Values may be sent and summed in bfloat16 or wider, within the bound.
A program may use at most 256 MiB of HBM per device.

v0:
```python
import jax
import jax.numpy as jnp
from jax import lax
from jax.sharding import PartitionSpec as P


def spread(value, axis, root):
    mine = lax.axis_index(axis) == root
    return lax.psum(jnp.where(mine, value, jnp.zeros_like(value)), axis)


def from_behind(block, axis, distance):
    devices = range(lax.axis_size(axis))
    route = [(i - distance, i) for i in devices if i - distance in devices]
    return lax.ppermute(block, axis, route)


def lag_table(out_rows, all_rows, offset_rows, tap_total):
    lags = (
        offset_rows
        + jnp.arange(out_rows, dtype=jnp.int32)[:, None]
        - jnp.arange(all_rows, dtype=jnp.int32)[None, :]
    )
    return (lags[:, :, None] == jnp.arange(tap_total, dtype=jnp.int32)[None, None, :]).astype(
        jnp.float32
    )


def build_toeplitz(long_row, onehot):
    return jnp.einsum("tsj,jg->gts", onehot, long_row, precision=lax.Precision.HIGHEST)


def fold_toeplitz(toep_grad, onehot):
    return jnp.einsum("tsj,gts->jg", onehot, toep_grad, precision=lax.Precision.HIGHEST)


def filters_apply(joined, normed, short_row, toep, offset_rows):
    count_rows = joined.shape[0]
    channels = joined.shape[1]
    groups_here = toep.shape[0]
    tap_count = short_row.shape[0]
    padded = jnp.pad(normed, ((tap_count - 1, 0), (0, 0)))
    shorter = jnp.zeros_like(normed)
    for offset in range(tap_count):
        begin = tap_count - 1 - offset
        shorter = shorter + short_row[offset][None, :] * padded[begin : begin + count_rows]
    grouped = shorter.reshape(count_rows, groups_here, channels // groups_here)
    longer = jnp.einsum("gts,sgk->tgk", toep, grouped, precision=lax.Precision.HIGHEST)
    longer = longer.reshape(toep.shape[1], channels)
    return joined[offset_rows:] + normed[offset_rows:] * longer


def mixer(comp_rows, prompt_rows, gain_row, short_row, toep):
    joined = jnp.concatenate([prompt_rows, comp_rows], axis=0).astype(jnp.float32)
    factor = lax.rsqrt(jnp.mean(joined * joined, axis=1, keepdims=True) + 1e-06)
    normed = joined * factor * gain_row[None, :]
    return filters_apply(joined, normed, short_row, toep, prompt_rows.shape[0])


def pair_slopes(table, pair_index):
    labels = jnp.arange(table.shape[1], dtype=jnp.int32)
    winner = (pair_index[:, :, 0:1] == labels).astype(jnp.float32)
    loser = (pair_index[:, :, 1:2] == labels).astype(jnp.float32)
    margin = jnp.sum((winner - loser) * table[:, None, :], axis=2)
    weight = jax.nn.sigmoid(-margin)
    return jnp.sum((loser - winner) * weight[:, :, None], axis=1)


def cotangent_rows(slope_arg, head_arg, length_arg, count_rows):
    live = (jnp.arange(count_rows, dtype=jnp.int32) < length_arg).astype(jnp.float32)
    return slope_arg * live[:, None] * head_arg[None, :] / jnp.sqrt(length_arg.astype(jnp.float32))


def score_rows(section_out, head_arg, length_arg):
    per_row = jnp.dot(section_out.astype(jnp.float32), head_arg, precision=lax.Precision.HIGHEST)
    live = jnp.arange(section_out.shape[0], dtype=jnp.int32) < length_arg
    return jnp.sum(jnp.where(live, per_row, 0.0)) / jnp.sqrt(length_arg.astype(jnp.float32))


def put_slot(stored, fresh, chosen, active):
    former = lax.dynamic_index_in_dim(stored, chosen, 0, keepdims=False)
    return lax.dynamic_update_index_in_dim(stored, jnp.where(active, fresh, former), chosen, 0)


def sectioned_run(
    completion_rows,
    prompt_pool,
    norm_gain,
    short_taps,
    long_taps,
    score_head,
    live_lengths,
    prompt_owner,
    pair_index,
):
    sections = lax.axis_size("section")
    section_id = lax.axis_index("section")
    micro_count = completion_rows.shape[0]
    comp_len = completion_rows.shape[2]
    feat_width = completion_rows.shape[3]
    tick_count = sections + micro_count - 1
    gain_row = norm_gain[0]
    short_row = short_taps[0]
    long_row = long_taps[0]
    own_rows = completion_rows[:, 0]
    own_lengths = live_lengths[:, 0]
    local_prompt = prompt_pool[0, 0]
    prompt_len = local_prompt.shape[0]
    is_last = section_id == sections - 1
    is_first = section_id == 0
    batch_labels = jnp.arange(micro_count, dtype=jnp.int32)
    onehot = lag_table(comp_len, prompt_len + comp_len, prompt_len, long_row.shape[0])
    toep = build_toeplitz(long_row, onehot)
    prompt_store = jnp.zeros((micro_count,) + local_prompt.shape, local_prompt.dtype)
    saved_rows = jnp.zeros_like(own_rows)
    own_scores = jnp.zeros((micro_count,), jnp.float32)
    received = jnp.zeros((comp_len, feat_width), jnp.bfloat16)
    for moment in range(tick_count):
        slot_raw = moment - section_id
        active = (slot_raw >= 0) & (slot_raw < micro_count)
        chosen = jnp.clip(slot_raw, 0, micro_count - 1)
        fresh = lax.dynamic_index_in_dim(own_rows, chosen, 0, keepdims=False)
        current = jnp.where(is_first, fresh, received)
        saved_rows = put_slot(saved_rows, current, chosen, active)
        prompt_now = spread(local_prompt, "resp", prompt_owner[chosen])
        prompt_store = put_slot(prompt_store, prompt_now, chosen, active)

        def run_layer():
            return mixer(current, prompt_now, gain_row, short_row, toep).astype(jnp.bfloat16)

        def skip_layer():
            return jnp.zeros((comp_len, feat_width), jnp.bfloat16)

        output = lax.cond(active, run_layer, skip_layer)
        score_now = score_rows(output, score_head, own_lengths[chosen])
        own_scores = jnp.where(active & is_last & (batch_labels == chosen), score_now, own_scores)
        if moment + 1 < tick_count:
            received = from_behind(output, "section", 1)
    table = lax.all_gather(own_scores[:, None], "resp", axis=1, tiled=True)
    slopes = pair_slopes(table, pair_index)
    own_slope = lax.dynamic_slice_in_dim(slopes, lax.axis_index("resp"), 1, 1)[:, 0]
    rounded_scores = own_scores.astype(jnp.bfloat16)
    grad_gain = jnp.zeros_like(gain_row)
    grad_short = jnp.zeros_like(short_row)
    toep_acc = jnp.zeros_like(toep)
    received_grad = jnp.zeros((comp_len, feat_width), jnp.bfloat16)
    known = rounded_scores
    for moment in range(tick_count):
        slot_raw = moment - (sections - 1 - section_id)
        active = (slot_raw >= 0) & (slot_raw < micro_count)
        chosen = jnp.clip(slot_raw, 0, micro_count - 1)
        rows_now = lax.dynamic_index_in_dim(saved_rows, chosen, 0, keepdims=False)
        prompt_now = lax.dynamic_index_in_dim(prompt_store, chosen, 0, keepdims=False)
        head_grad = cotangent_rows(own_slope[chosen], score_head, own_lengths[chosen], comp_len)
        upstream = jnp.where(is_last, head_grad, received_grad.astype(jnp.float32))

        def pull_back():

            def local_layer(rows_var, gain_var, short_var, toep_var):
                return mixer(rows_var, prompt_now, gain_var, short_var, toep_var)

            primal, puller = jax.vjp(local_layer, rows_now, gain_row, short_row, toep)
            return puller(upstream)

        def nothing_back():
            return (
                jnp.zeros((comp_len, feat_width), jnp.bfloat16),
                jnp.zeros_like(gain_row),
                jnp.zeros_like(short_row),
                jnp.zeros_like(toep),
            )

        grad_rows, step_gain, step_short, step_toep = lax.cond(active, pull_back, nothing_back)
        toep_acc = toep_acc + step_toep
        grad_gain = grad_gain + step_gain
        grad_short = grad_short + step_short
        if moment + 1 < tick_count:
            received_grad, passed_scores = from_behind((grad_rows, known), "section", -1)
            known = jnp.where(is_last, rounded_scores, passed_scores)
    grad_long = fold_toeplitz(toep_acc, onehot)
    grad_gain, grad_short, grad_long = lax.psum((grad_gain, grad_short, grad_long), "resp")
    return (known[:, None], grad_gain[None], grad_short[None], grad_long[None])


def body(
    completion_rows,
    prompt_pool,
    norm_gain,
    short_taps,
    long_taps,
    score_head,
    live_lengths,
    prompt_owner,
    pair_index,
):
    results = sectioned_run(
        completion_rows,
        prompt_pool,
        norm_gain,
        short_taps,
        long_taps,
        score_head,
        live_lengths,
        prompt_owner,
        pair_index,
    )
    return results


def solution(mesh):
    placed = (
        P(None, ("groups", "resp"), None, None),
        P("section", ("groups", "resp"), None, None),
        P("section", None),
        P("section", None, None),
        P("section", None, None),
        P(),
        P(None, ("groups", "resp")),
        P("groups"),
        P(None, "groups", None),
    )
    return jax.shard_map(
        body,
        mesh=mesh,
        in_specs=placed,
        out_specs=(
            P(None, ("groups", "resp")),
            P("section", "groups"),
            P("section", "groups", None),
            P("section", "groups", None),
        ),
        check_vma=False,
    )
```

profile of v0, /device:TPU:0, one launch (start us, length us, event | category | flops | bytes accessed | tf_op | source)
XLA Modules:
  0.0 1085.9 jit_solution(16352563520942501082)
XLA Ops:
  29.0 94.0 %all-reduce.96.cloned.1.call-done = (bf16[64,4096]{1,0:T(8,128)(2,1)}, bf16[64,4096]{1,0:T(8,128)(2,1)}, bf16[64,4096]{1,0:T(8,128)(2,1)}, bf16[64,4096]{1,0:T(8,128)(2,1)}, bf16[64,4096]{1,0:T(8,128)(2,1)}) async-done(((bf16[64,4096]{1,0:T(8,128)(2,1)}, bf16[64,4096]{1,0:T(8,128)(2,1)}, bf16[64,4096]{1,0:T(8,128)(2,1)}, bf16[64,4096]{1,0:T(8,128)(2,1)}, bf16[64,4096]{1,0:T(8,128)(2,1)}), ...) | async-done | bytes 2621456 | tf_op jit(solution)/shard_map/psum | solution.py:9
  124.9 43.3 %conditional.10 = (bf16[64,4096]{0,1:T(8,128)(2,1)}) conditional(s32[]{:T(128)} %convert_element_type.230, () %tuple.107, (pred[]{:T(512)}, bf16[1,1,64,4096]{3,2,1,0:T(8,128)(2,1)S(1)}, bf16[64,4096]{1,0:T(8,128)(2,1)S(1)}, bf16[64,4096]{1,0:T(8,128)(2,1)}, f32[1,4096]{1,0:T(1,128)S(1)}, /*index=5*/f32[7,4096]{1,0:T(8,128)S(1)}, ...), branch_computations={%region_5.6_spmd, %region_6.8_spmd} | conditional | flops 418906240 | bytes 61179996 | solution.py:134
  150.2 15.8 %fusion.174 = f32[256,16,64]{2,1,0:T(8,128)S(1)} fusion(f32[128,256,16]{0,2,1:T(8,128)} %bitcast.617, f32[256,64,128]{2,1,0:T(8,128)} %copy.120), kind=kOutput, calls=%fused_computation.529 | convolution fusion | flops 402653184 | bytes 11534336 | tf_op jit(solution)/shard_map/cond/branch_1_fun/gts,sgk->tgk/dot_general | solution.py:48
  170.6 13.7 %collective-permute-start = (bf16[64,4096]{1,0:T(8,128)(2,1)}, bf16[64,4096]{1,0:T(8,128)(2,1)}, u32[]{:S(2)}, u32[]{:S(2)}) collective-permute-start(bf16[64,4096]{1,0:T(8,128)(2,1)} %copy.121), channel_id=1, source_target_pairs={{0,1},{1,2},{2,3},{4,5},{5,6},{6,7},{8,9},{9,10},{10,11},{12,13},{... | collective-permute-start | bytes 1572872 | tf_op jit(solution)/shard_map/ppermute | solution.py:15
  214.8 43.1 %conditional.11 = (bf16[64,4096]{0,1:T(8,128)(2,1)S(1)}) conditional(s32[]{:T(128)} %convert_element_type.229, () %tuple.106, (bf16[64,4096]{1,0:T(8,128)(2,1)}, bf16[64,4096]{1,0:T(8,128)(2,1)}, f32[1,4096]{1,0:T(1,128)S(1)}, f32[7,4096]{1,0:T(8,128)S(1)}, f32[256,64,128]{0,2,1:T(8,128)}) %tuple.377), branch_computations={%region_8.9_spmd, %region_9.11_spmd} | conditional | flops 418644096 | bytes 73238648 | solution.py:134
  240.9 15.8 %fusion.175 = f32[256,16,64]{2,1,0:T(8,128)S(1)} fusion(f32[128,256,16]{0,2,1:T(8,128)} %bitcast.618, f32[256,64,128]{2,1,0:T(8,128)} %copy.124), kind=kOutput, calls=%fused_computation.530 | convolution fusion | flops 402653184 | bytes 11534336 | tf_op jit(solution)/shard_map/cond/branch_1_fun/gts,sgk->tgk/dot_general | solution.py:48
  274.7 40.2 %collective-permute-start.2 = (bf16[64,4096]{1,0:T(8,128)(2,1)}, bf16[64,4096]{1,0:T(8,128)(2,1)}, u32[]{:S(2)}, u32[]{:S(2)}) collective-permute-start(bf16[64,4096]{1,0:T(8,128)(2,1)} %copy.129), channel_id=1, source_target_pairs={{0,1},{1,2},{2,3},{4,5},{5,6},{6,7},{8,9},{9,10},{10,11},{12,13},{... | collective-permute-start | bytes 1572872 | tf_op jit(solution)/shard_map/ppermute | solution.py:15
  360.8 15.7 %conditional.15 = (bf16[64,4096]{0,1:T(8,128)(2,1)}, f32[4096]{0:T(1024)S(1)}, f32[7,4096]{1,0:T(8,128)S(1)}, f32[256,64,128]{2,1,0:T(8,128)}) conditional(s32[]{:T(128)} %convert_element_type.237, () %tuple.113, (s32[]{:T(128)}, s32[2,1]{0,1:T(1,128)S(1)}, s32[64,1]{0,1:T(1,128)S(1)}, f32[2,4]{1,0:T(2,128)S(1)}, s32[]{:T(128)}, ...), branch_computations={%region_27.28_spmd, %region_28.39_spmd} | conditional | flops 1245062016 | bytes 171630560 | solution.py:173
  380.7 44.2 %collective-permute-done.8 = bf16[64,4096]{1,0:T(8,128)(2,1)} collective-permute-done((bf16[64,4096]{1,0:T(8,128)(2,1)S(1)}, bf16[64,4096]{1,0:T(8,128)(2,1)}, u32[]{:S(2)}, u32[]{:S(2)}) %collective-permute-start.8) | collective-permute-done | bytes 524320 | tf_op jit(solution)/shard_map/ppermute | solution.py:15
  427.0 15.6 %conditional.16 = (bf16[64,4096]{0,1:T(8,128)(2,1)}, f32[4096]{0:T(1024)S(1)}, f32[7,4096]{1,0:T(8,128)S(1)}, f32[256,64,128]{2,1,0:T(8,128)}) conditional(s32[]{:T(128)} %convert_element_type.240, () %tuple.115, (s32[]{:T(128)}, s32[2,1]{0,1:T(1,128)S(1)}, s32[64,1]{0,1:T(1,128)S(1)}, f32[2,4]{1,0:T(2,128)S(1)}, s32[]{:T(128)}, ...), branch_computations={%region_39.40_spmd, %region_40.51_spmd} | conditional | flops 1245062016 | bytes 174776288 | solution.py:173
  460.2 15.6 %conditional.17 = (bf16[64,4096]{0,1:T(8,128)(2,1)}, f32[4096]{0:T(1024)S(1)}, f32[7,4096]{1,0:T(8,128)S(1)}, f32[256,64,128]{2,1,0:T(8,128)}) conditional(s32[]{:T(128)} %convert_element_type.242, () %tuple.117, (s32[]{:T(128)}, s32[2,1]{0,1:T(1,128)S(1)}, s32[64,1]{0,1:T(1,128)S(1)}, f32[2,4]{1,0:T(2,128)S(1)}, s32[]{:T(128)}, ...), branch_computations={%region_51.52_spmd, %region_52.0_spmd} | conditional | flops 1245062016 | bytes 174776288 | solution.py:173
  481.3 296.5 %collective-permute-done.10 = bf16[64,4096]{1,0:T(8,128)(2,1)} collective-permute-done((bf16[64,4096]{1,0:T(8,128)(2,1)S(1)}, bf16[64,4096]{1,0:T(8,128)(2,1)}, u32[]{:S(2)}, u32[]{:S(2)}) %collective-permute-start.10) | collective-permute-done | bytes 524320 | tf_op jit(solution)/shard_map/ppermute | solution.py:15
  779.8 101.2 %conditional.18 = (bf16[64,4096]{0,1:T(8,128)(2,1)}, f32[4096]{0:T(1024)S(1)}, f32[7,4096]{1,0:T(8,128)S(1)}, f32[256,64,128]{2,1,0:T(8,128)}) conditional(s32[]{:T(128)} %convert_element_type.244, () %tuple.119, (s32[]{:T(128)}, s32[2,1]{0,1:T(1,128)S(1)}, s32[64,1]{0,1:T(1,128)S(1)}, f32[2,4]{1,0:T(2,128)S(1)}, s32[]{:T(128)}, ...), branch_computations={%region_63.64_spmd, %region_64.0_spmd} | conditional | flops 1245062016 | bytes 174776288 | solution.py:173
  801.8 16.7 %fusion.187 = f32[256,16,64]{2,1,0:T(8,128)} fusion(f32[128,256,16]{0,2,1:T(8,128)} %bitcast.583, f32[256,64,128]{2,1,0:T(8,128)} %copy.165), kind=kOutput, calls=%fused_computation.542 | convolution fusion | flops 402653184 | bytes 11534336 | tf_op jit(solution)/shard_map/cond/branch_1_fun/jvp(gts,sgk->tgk)/dot_general | solution.py:48
  844.5 11.8 %fusion.105 = (f32[4096]{0:T(1024)S(1)}, f32[4096]{0:T(1024)S(1)}, f32[4096]{0:T(1024)S(1)}, f32[4096]{0:T(1024)S(1)}, f32[4096]{0:T(1024)S(1)}, /*index=5*/f32[...) fusion(f32[256,16,128]{2,1,0:T(8,128)S(1)} %get-tuple-element.1, ...), kind=kLoop, calls=%fused_computation.333 | loop fusion | flops 9936896 | bytes 19087360 | tf_op jit(solution)/shard_map/cond/branch_1_fun/transpose(jvp())/reduce_sum | solution.py:46
  864.0 16.9 %fusion.188 = f32[256,64,128]{2,1,0:T(8,128)} fusion(f32[256,16,64]{2,1,0:T(8,128)} %bitcast.578, f32[128,256,16]{0,2,1:T(8,128)} %bitcast.584), kind=kOutput, calls=%fused_computation.543 | convolution fusion | flops 402653184 | bytes 11534336 | tf_op jit(solution)/shard_map/cond/branch_1_fun/transpose(jvp(gts,sgk->tgk))/dot_general | solution.py:48
  907.5 99.8 %conditional.19 = (f32[4096]{0:T(1024)S(1)}, f32[7,4096]{1,0:T(8,128)S(1)}, f32[256,64,128]{2,1,0:T(8,128)}) conditional(s32[]{:T(128)} %convert_element_type.246, () %tuple.121, (s32[]{:T(128)}, bf16[2,64,4096]{1,2,0:T(8,128)(2,1)}, bf16[2,64,4096]{1,2,0:T(8,128)(2,1)}, s32[2,1]{0,1:T(1,128)}, s32[64,1]{0,1:T(1,128)}, ...), branch_computations={%region_75.76_spmd, %region_76.86_spmd} | conditional | flops 1244012800 | bytes 143633472 | solution.py:173
  934.0 16.7 %fusion.179 = f32[256,16,64]{2,1,0:T(8,128)} fusion(f32[128,256,16]{0,2,1:T(8,128)} %bitcast.587, f32[256,64,128]{2,1,0:T(8,128)} %copy.168), kind=kOutput, calls=%fused_computation.534 | convolution fusion | flops 402653184 | bytes 11534336 | tf_op jit(solution)/shard_map/cond/branch_1_fun/jvp(gts,sgk->tgk)/dot_general | solution.py:48
  971.7 12.2 %fusion.119 = (f32[4096]{0:T(1024)}, f32[4096]{0:T(1024)}, f32[4096]{0:T(1024)}, f32[4096]{0:T(1024)}, f32[4096]{0:T(1024)}, /*index=5*/f32[4096]{0:T(1024)}, f3...) fusion(f32[256,16,128]{2,1,0:T(8,128)S(1)} %get-tuple-element.1, ...), kind=kLoop, calls=%fused_computation.392 | loop fusion | flops 9936896 | bytes 19087360 | tf_op jit(solution)/shard_map/cond/branch_1_fun/transpose(jvp())/reduce_sum | solution.py:46
  990.4 16.6 %fusion.180 = f32[256,64,128]{2,1,0:T(8,128)} fusion(f32[256,16,64]{2,1,0:T(8,128)} %bitcast.590, f32[128,256,16]{0,2,1:T(8,128)S(1)} %bitcast.588), kind=kOutput, calls=%fused_computation.535 | convolution fusion | flops 402653184 | bytes 11534336 | tf_op jit(solution)/shard_map/cond/branch_1_fun/transpose(jvp(gts,sgk->tgk))/dot_general | solution.py:48
  1009.2 19.7 %add_add_fusion.4 = f32[256,64,128]{2,1,0:T(8,128)} fusion(f32[256,64,128]{2,1,0:T(8,128)} %get-tuple-element.909, f32[256,64,128]{2,1,0:T(8,128)} %get-tuple-element.908, f32[256,64,128]{2,1,0:T(8,128)} %get-tuple-element.907, f32[256,64,128]{2,1,0:T(8,128)} %get-tuple-element.905, f32[256,64,128]{2,1,0:T(8,128)} %get-tuple-element.906), kind=kLoop, calls=%fused_computation.412 | loop fusion | flops 8388608 | bytes 50331648 | tf_op jit(solution)/shard_map/add | solution.py:174
  1029.0 13.8 %fusion.133 = f32[1,128,256]{2,1,0:T(8,128)} fusion(f32[256,64,128]{2,1,0:T(8,128)} %add_add_fusion.4, s32[64,128]{1,0:T(8,128)S(1)} %copy-done.89), kind=kOutput, calls=%fused_computation.418 | convolution fusion | flops 3222274048 | bytes 8552448 | tf_op jit(solution)/shard_map/tsj,gts->jg/dot_general | solution.py:34
  1044.1 17.1 %psum.61 = f32[1,4096]{1,0:T(1,128)} all-reduce(f32[1,4096]{1,0:T(1,128)S(1)} %bitcast.746), channel_id=1, replica_groups=mesh['groups'=2,'resp'=4,'section'=4] {'resp'}, use_global_device_ids=true, to_apply=%region_86.87 | all-reduce | flops 4096 | bytes 32768 | tf_op jit(solution)/shard_map/psum | solution.py:181
  1061.2 14.6 %all-reduce.94.cloned.1.call-done = (f32[1,7,4096]{2,0,1:T(1,128)}, f32[1,128,256]{2,1,0:T(8,128)}) async-done(((f32[1,7,4096]{2,0,1:T(1,128)}, f32[1,128,256]{2,1,0:T(8,128)}), (f32[1,7,4096]{2,0,1:T(1,128)}, f32[1,128,256]{2,1,0:T(8,128)})) %all-reduce.94.cloned.1.call-update) | async-done | bytes 245776 | tf_op jit(solution)/shard_map/psum | solution.py:181
  (358 shorter events, 352.4 us)
Async XLA Ops:
  7.2 16.1 %copy-start = (f32[1,128,256]{2,1,0:T(8,128)S(1)}, f32[1,128,256]{2,1,0:T(8,128)}, u32[]{:S(2)}) copy-start(f32[1,128,256]{2,1,0:T(8,128)} %param.33) | copy-start | bytes 393220
  7.2 115.8 %all-reduce.96.cloned.1.call-start = ((), (), s32[]{:S(2)}) async-start(), calls=%async_computation.1 | async-start | bytes 5242880 | tf_op jit(solution)/shard_map/psum | solution.py:9
  14.6 1061.2 %all-reduce.94.cloned.1.call-start = ((), (), s32[]{:S(2)}) async-start(), calls=%async_computation | async-start | bytes 491520 | tf_op jit(solution)/shard_map/psum | solution.py:181
  23.3 101.7 %copy-start.80 = (f32[1,4096]{1,0:T(1,128)S(1)}, f32[1,4096]{1,0:T(1,128)}, u32[]{:S(2)}) copy-start(f32[1,4096]{1,0:T(1,128)} %param.31) | copy-start | bytes 49156
  170.6 39.4 %collective-permute-start = (bf16[64,4096]{1,0:T(8,128)(2,1)}, bf16[64,4096]{1,0:T(8,128)(2,1)}, u32[]{:S(2)}, u32[]{:S(2)}) collective-permute-start(bf16[64,4096]{1,0:T(8,128)(2,1)} %copy.121), channel_id=1, source_target_pairs={{0,1},{1,2},{2,3},{4,5},{5,6},{6,7},{8,9},{9,10},{10,11},{12,13},{... | collective-permute-start | bytes 1572872 | tf_op jit(solution)/shard_map/ppermute | solution.py:15
  240.8 15.8 %copy-start.18 = (f32[128,4096]{0,1:T(8,128)S(1)}, f32[128,4096]{0,1:T(8,128)}, u32[]{:S(2)}) copy-start(f32[128,4096]{0,1:T(8,128)} %copy-done.17) | copy-start | bytes 6291460 | tf_op jit(solution)/shard_map/cond
  240.8 15.9 %copy-start.67 = (f32[128,4096]{0,1:T(8,128)S(1)}, f32[128,4096]{0,1:T(8,128)}, u32[]{:S(2)}) copy-start(f32[128,4096]{0,1:T(8,128)} %maximum_convert_fusion.1) | copy-start | bytes 6291460 | tf_op jit(solution)/shard_map/cond
  259.0 9.1 collective-permute-start.1
  274.7 47.3 %collective-permute-start.2 = (bf16[64,4096]{1,0:T(8,128)(2,1)}, bf16[64,4096]{1,0:T(8,128)(2,1)}, u32[]{:S(2)}, u32[]{:S(2)}) collective-permute-start(bf16[64,4096]{1,0:T(8,128)(2,1)} %copy.129), channel_id=1, source_target_pairs={{0,1},{1,2},{2,3},{4,5},{5,6},{6,7},{8,9},{9,10},{10,11},{12,13},{... | collective-permute-start | bytes 1572872 | tf_op jit(solution)/shard_map/ppermute | solution.py:15
  328.4 9.2 collective-permute-start.3
  356.3 423.5 %copy-start.118 = (f32[2,4]{1,0:T(2,128)}, f32[2,4]{1,0:T(2,128)S(1)}, u32[]{:S(2)}) copy-start(f32[2,4]{1,0:T(2,128)S(1)} %fusion.156) | copy-start | bytes 100
  360.8 419.0 %copy-start.114 = (f32[64,1]{0,1:T(1,128)}, f32[64,1]{0,1:T(1,128)S(1)}, u32[]{:S(2)}) copy-start(f32[64,1]{0,1:T(1,128)S(1)} %broadcast.837) | copy-start | bytes 772
  379.4 45.5 %collective-permute-start.8 = (bf16[64,4096]{1,0:T(8,128)(2,1)S(1)}, bf16[64,4096]{1,0:T(8,128)(2,1)}, u32[]{:S(2)}, u32[]{:S(2)}) collective-permute-start(bf16[64,4096]{1,0:T(8,128)(2,1)S(1)} %copy.157), channel_id=1, source_target_pairs={{1,0},{2,1},{3,2},{5,4},{6,5},{7,6},{9,8},{10,9},{11,10},{13,12},{... | collective-permute-start | bytes 1572872 | tf_op jit(solution)/shard_map/ppermute | solution.py:15
  445.4 12.7 %collective-permute-start.9 = (bf16[64,4096]{1,0:T(8,128)(2,1)S(1)}, bf16[64,4096]{1,0:T(8,128)(2,1)}, u32[]{:S(2)}, u32[]{:S(2)}) collective-permute-start(bf16[64,4096]{1,0:T(8,128)(2,1)S(1)} %copy.160), channel_id=1, source_target_pairs={{1,0},{2,1},{3,2},{5,4},{6,5},{7,6},{9,8},{10,9},{11,10},{13,12},{... | collective-permute-start | bytes 1572872 | tf_op jit(solution)/shard_map/ppermute | solution.py:15
  478.6 299.1 %collective-permute-start.10 = (bf16[64,4096]{1,0:T(8,128)(2,1)S(1)}, bf16[64,4096]{1,0:T(8,128)(2,1)}, u32[]{:S(2)}, u32[]{:S(2)}) collective-permute-start(bf16[64,4096]{1,0:T(8,128)(2,1)S(1)} %copy.163), channel_id=1, source_target_pairs={{1,0},{2,1},{3,2},{5,4},{6,5},{7,6},{9,8},{10,9},{11,10},{13,12},{... | collective-permute-start | bytes 1572872 | tf_op jit(solution)/shard_map/ppermute | solution.py:15
  480.0 405.2 %collective-permute-start.4 = (bf16[2]{0:T(256)(128)(2,1)S(1)}, bf16[2]{0:T(256)(128)(2,1)S(1)}, u32[]{:S(2)}, u32[]{:S(2)}) collective-permute-start(bf16[2]{0:T(256)(128)(2,1)S(1)} %fusion.160), channel_id=1, source_target_pairs={{1,0},{2,1},{3,2},{5,4},{6,5},{7,6},{9,8},{10,9},{11,10},{13,12},{... | collective-permute-start | bytes 20 | tf_op jit(solution)/shard_map/ppermute | solution.py:15
  883.9 22.1 %collective-permute-start.11 = (bf16[64,4096]{1,0:T(8,128)(2,1)S(1)}, bf16[64,4096]{1,0:T(8,128)(2,1)S(1)}, u32[]{:S(2)}, u32[]{:S(2)}) collective-permute-start(bf16[64,4096]{1,0:T(8,128)(2,1)S(1)} %copy.166), channel_id=1, source_target_pairs={{1,0},{2,1},{3,2},{5,4},{6,5},{7,6},{9,8},{10,9},{11,10},{13,12},{... | collective-permute-start | bytes 1572872 | tf_op jit(solution)/shard_map/ppermute | solution.py:15
  885.2 10.3 collective-permute-start.5
  895.5 8.6 collective-permute-start.6
  904.6 138.2 %collective-permute-start.7 = (bf16[2]{0:T(256)(128)(2,1)}, bf16[2]{0:T(256)(128)(2,1)}, u32[]{:S(2)}, u32[]{:S(2)}) collective-permute-start(bf16[2]{0:T(256)(128)(2,1)} %broadcast_select_fusion.1), channel_id=1, source_target_pairs={{1,0},{2,1},{3,2},{5,4},{6,5},{7,6},{9,8},{10,9},{11,10},{13,12},{... | collective-permute-start | bytes 20 | tf_op jit(solution)/shard_map/ppermute | solution.py:15
  907.5 99.8 %copy-start.84 = (f32[7,4096]{1,0:T(8,128)S(1)}, f32[7,4096]{1,0:T(8,128)}, u32[]{:S(2)}) copy-start(f32[7,4096]{1,0:T(8,128)} %copy-done.83) | copy-start | bytes 344068
  990.3 16.6 %copy-start.111 = (f32[4096]{0:T(1024)S(1)}, f32[4096]{0:T(1024)}, u32[]{:S(2)}) copy-start(f32[4096]{0:T(1024)} %fusion.116) | copy-start | bytes 49156 | tf_op jit(solution)/shard_map/cond
  1009.2 19.7 %copy-start.89 = (s32[64,128]{1,0:T(8,128)S(1)}, s32[64,128]{1,0:T(8,128)}, u32[]{:S(2)}) copy-start(s32[64,128]{1,0:T(8,128)} %copy-done.88) | copy-start | bytes 98308
  1029.0 49.9 %copy-start.1 = (f32[1,128,256]{2,1,0:T(8,128)S(1)}, f32[1,128,256]{2,1,0:T(8,128)}, u32[]{:S(2)}) copy-start(f32[1,128,256]{2,1,0:T(8,128)} %param.33) | copy-start | bytes 393220
  (66 other events, 408.1 us)
Sparse Core Ops, SparseCore 0:
  14.7 108.2 all-reduce.95
  1042.9 32.8 all-reduce.93
where the time goes:
time: 1090 us
  waiting for transfers between devices  477 us (44%)
  other arithmetic  157 us (14%)
  matrix products  151 us (14%)
  local copies, waits for them, and re-layouts  148 us (14%)
  starting transfers between devices  68.4 us (6%)
  loops' own time  34.5 us (3%)
  blocking collectives  25.6 us (2%)
  between operations  24.9 us (2%)
    ppermute x12, waiting for transfers between devices, from_behind(): return lax.ppermute(block, axis, route)  368 us
    dot_general x8, matrix products, filters_apply(): jnp.einsum('gts,sgk->tgk', toep, grouped, precision=lax.Precision.HIGHEST)  120 us
    psum x1, waiting for transfers between devices, spread(): return lax.psum(jnp.where(mine, value, jnp.zeros_like(value)), axis)  94 us
    ppermute x12, starting transfers between devices, from_behind(): return lax.ppermute(block, axis, route)  68.4 us
    another operation x32, local copies, waits for them, and re-layouts  67.1 us
    add x4, other arithmetic, filters_apply(): shorter + short_row[offset][None, :] * padded[begin:begin + count_rows]  33.5 us
    another operation x5, loops' own time, sectioned_run(): lax.cond(active, pull_back, nothing_back)  33.2 us
    reduce_sum x2, other arithmetic, filters_apply(): short_row[offset][None, :] * padded[begin:begin + count_rows]  24 us
  transfers between devices with their start and end apart: 14, of which 7 were waited for; matrix products, arithmetic and copies ran while one was open for 27% of the time, Pallas kernels for 0%

commit v1 on v0

--- a/solution.py
+++ b/solution.py
@@ -3,10 +3,12 @@
 from jax import lax
 from jax.sharding import PartitionSpec as P
 
+lay_the_paths = lambda view, row_axis: lax.all_gather(view, row_axis).sum(axis=0)
+
 
 def spread(value, axis, root):
     mine = lax.axis_index(axis) == root
-    return lax.psum(jnp.where(mine, value, jnp.zeros_like(value)), axis)
+    return lay_the_paths(jnp.where(mine, value, jnp.zeros_like(value)), axis)
 
 
 def from_behind(block, axis, distance):

time: 1090 us -> 1150 us (1.055)
  waiting for transfers between devices: 477 us -> 563 us
  local copies, waits for them, and re-layouts: 148 us -> 114 us
    all_gather x0 -> x5, waiting for transfers between devices: none -> 155 us  [lax.all_gather(view, row_axis).sum(axis=0)]
    psum x1 -> x0, waiting for transfers between devices: 94 us -> none  [spread(): return lax.psum(jnp.where(mine, value, jnp.zeros_like(value)), axis)]
    ppermute x12, waiting for transfers between devices: 368 us -> 391 us  [from_behind(): return lax.ppermute(block, axis, route)]
    dynamic_slice x16 -> x4, local copies, waits for them, and re-layouts: 20.1 us -> 0.99 us  [put_slot(): former = lax.dynamic_index_in_dim(stored, chosen, 0, keepdims=False)]
    broadcast_in_dim x9 -> x0, other arithmetic: 18.8 us -> none  [put_slot(): lax.dynamic_update_index_in_dim(stored, jnp.where(active, fresh, former),...]
    broadcast_in_dim x9 -> x0, local copies, waits for them, and re-layouts: 15.4 us -> none  [put_slot(): lax.dynamic_update_index_in_dim(stored, jnp.where(active, fresh, former),...]
    reduce_sum x0 -> x5, other arithmetic: none -> 13.6 us  [lax.all_gather(view, row_axis).sum(axis=0)]
    dynamic_update_slice x0 -> x10, other arithmetic: none -> 12.5 us  [put_slot(): lax.dynamic_update_index_in_dim(stored, jnp.where(active, fresh, former),...]
  transfers between devices with their start and end apart: 14 -> 18, of which waited for: 7 -> 10; matrix products, arithmetic and copies ran while one was open for 27% -> 29% of each run, Pallas kernels for 0% -> 0%
where the time goes in v1:
time: 1150 us
  waiting for transfers between devices  563 us (49%)
  other arithmetic  164 us (14%)
  matrix products  152 us (13%)
  local copies, waits for them, and re-layouts  114 us (10%)
  starting transfers between devices  72.8 us (6%)
  loops' own time  28.9 us (3%)
  blocking collectives  25.6 us (2%)
  between operations  25 us (2%)
    ppermute x12, waiting for transfers between devices, from_behind(): return lax.ppermute(block, axis, route)  391 us
    all_gather x5, waiting for transfers between devices, lax.all_gather(view, row_axis).sum(axis=0)  155 us
    dot_general x8, matrix products, filters_apply(): jnp.einsum('gts,sgk->tgk', toep, grouped, precision=lax.Precision.HIGHEST)  121 us
    another operation x34, local copies, waits for them, and re-layouts  77.6 us
    ppermute x12, starting transfers between devices, from_behind(): return lax.ppermute(block, axis, route)  72.6 us
    add x4, other arithmetic, filters_apply(): shorter + short_row[offset][None, :] * padded[begin:begin + count_rows]  33.6 us
    another operation x5, loops' own time, sectioned_run(): lax.cond(active, pull_back, nothing_back)  27.4 us
    reduce_sum x2, other arithmetic, filters_apply(): short_row[offset][None, :] * padded[begin:begin + count_rows]  23.4 us
  transfers between devices with their start and end apart: 18, of which 10 were waited for; matrix products, arithmetic and copies ran while one was open for 29% of the time, Pallas kernels for 0%

profile of v1, /device:TPU:0, one launch (start us, length us, event | category | flops | bytes accessed | tf_op | source)
XLA Modules:
  0.0 1145.5 jit_solution(1085544235015009280)
XLA Ops:
  29.3 33.9 %all-gather.20.cloned.1.call-done = bf16[4,1,64,4096]{3,2,1,0:T(8,128)(2,1)} async-done(((bf16[1,1,64,4096]{3,2,1,0:T(8,128)(2,1)}), bf16[4,1,64,4096]{3,2,1,0:T(8,128)(2,1)}) %all-gather.20.cloned.1.call-update) | async-done | bytes 2097168 | tf_op jit(solution)/shard_map/all_gather | solution.py:6
  66.1 43.5 %conditional.10 = (bf16[64,4096]{0,1:T(8,128)(2,1)}) conditional(s32[]{:T(128)} %convert_element_type.240, () %tuple.107, (pred[]{:T(512)}, bf16[1,1,64,4096]{3,2,1,0:T(8,128)(2,1)S(1)}, bf16[64,4096]{1,0:T(8,128)(2,1)}, f32[1,4096]{1,0:T(1,128)S(1)}, f32[7,4096]{1,0:T(8,128)S(1)}, /*index=5*/f32[256,64,128]{0,2,1:T(8,128)}) %tuple.403), branch_computations={%region_5.6_spmd, %region_6.8_spmd} | conditional | flops 418906240 | bytes 63801492 | solution.py:136
  91.6 15.8 %fusion.170 = f32[256,16,64]{2,1,0:T(8,128)S(1)} fusion(f32[128,256,16]{0,2,1:T(8,128)} %bitcast.599, f32[256,64,128]{2,1,0:T(8,128)} %copy.150), kind=kOutput, calls=%fused_computation.515 | convolution fusion | flops 402653184 | bytes 11534336 | tf_op jit(solution)/shard_map/cond/branch_1_fun/gts,sgk->tgk/dot_general | solution.py:50
  120.8 35.0 %all-gather.16.cloned.1.call-done = bf16[4,1,64,4096]{3,2,1,0:T(8,128)(2,1)} async-done(((bf16[1,1,64,4096]{3,2,1,0:T(8,128)(2,1)}), bf16[4,1,64,4096]{3,2,1,0:T(8,128)(2,1)}) %all-gather.16.cloned.1.call-update) | async-done | bytes 2097168 | tf_op jit(solution)/shard_map/all_gather | solution.py:6
  157.9 44.1 %all-gather.14.cloned.1.call-done = bf16[4,1,64,4096]{3,2,1,0:T(8,128)(2,1)} async-done(((bf16[1,1,64,4096]{3,2,1,0:T(8,128)(2,1)}), bf16[4,1,64,4096]{3,2,1,0:T(8,128)(2,1)}) %all-gather.14.cloned.1.call-update) | async-done | bytes 2097168 | tf_op jit(solution)/shard_map/all_gather | solution.py:6
  206.5 41.6 %all-gather.12.cloned.1.call-done = bf16[4,1,64,4096]{3,2,1,0:T(8,128)(2,1)} async-done(((bf16[1,1,64,4096]{3,2,1,0:T(8,128)(2,1)}), bf16[4,1,64,4096]{3,2,1,0:T(8,128)(2,1)}) %all-gather.12.cloned.1.call-update) | async-done | bytes 2097168 | tf_op jit(solution)/shard_map/all_gather | solution.py:6
  254.3 43.0 %conditional.11 = (bf16[64,4096]{0,1:T(8,128)(2,1)S(1)}) conditional(s32[]{:T(128)} %convert_element_type.239, () %tuple.106, (bf16[64,4096]{1,0:T(8,128)(2,1)}, bf16[64,4096]{1,0:T(8,128)(2,1)}, f32[1,4096]{1,0:T(1,128)S(1)}, f32[7,4096]{1,0:T(8,128)S(1)}, f32[256,64,128]{0,2,1:T(8,128)}) %tuple.393), branch_computations={%region_8.9_spmd, %region_9.11_spmd} | conditional | flops 418644096 | bytes 73238648 | solution.py:136
  280.3 15.8 %fusion.171 = f32[256,16,64]{2,1,0:T(8,128)S(1)} fusion(f32[128,256,16]{0,2,1:T(8,128)} %bitcast.600, f32[256,64,128]{2,1,0:T(8,128)} %copy.154), kind=kOutput, calls=%fused_computation.516 | convolution fusion | flops 402653184 | bytes 11534336 | tf_op jit(solution)/shard_map/cond/branch_1_fun/gts,sgk->tgk/dot_general | solution.py:50
  307.4 48.9 %collective-permute-start.2 = (bf16[64,4096]{1,0:T(8,128)(2,1)}, bf16[64,4096]{1,0:T(8,128)(2,1)}, u32[]{:S(2)}, u32[]{:S(2)}) collective-permute-start(bf16[64,4096]{1,0:T(8,128)(2,1)} %copy.159), channel_id=1, source_target_pairs={{0,1},{1,2},{2,3},{4,5},{5,6},{6,7},{8,9},{9,10},{10,11},{12,13},{... | collective-permute-start | bytes 1572872 | tf_op jit(solution)/shard_map/ppermute | solution.py:17
  393.9 14.3 %conditional.15 = (bf16[64,4096]{0,1:T(8,128)(2,1)}, f32[4096]{0:T(1024)S(1)}, f32[7,4096]{1,0:T(8,128)}, f32[256,64,128]{2,1,0:T(8,128)}) conditional(s32[]{:T(128)} %convert_element_type.247, () %tuple.113, (s32[]{:T(128)}, s32[2,1]{0,1:T(1,128)S(1)}, s32[64,1]{0,1:T(1,128)S(1)}, f32[2,4]{1,0:T(2,128)S(1)}, s32[]{:T(128)}, ...), branch_computations={%region_27.28_spmd, %region_28.39_spmd} | conditional | flops 1245062016 | bytes 176292192 | solution.py:175
  411.9 49.0 %collective-permute-done.8 = bf16[64,4096]{1,0:T(8,128)(2,1)} collective-permute-done((bf16[64,4096]{1,0:T(8,128)(2,1)}, bf16[64,4096]{1,0:T(8,128)(2,1)}, u32[]{:S(2)}, u32[]{:S(2)}) %collective-permute-start.8) | collective-permute-done | bytes 524320 | tf_op jit(solution)/shard_map/ppermute | solution.py:17
  462.9 14.3 %conditional.16 = (bf16[64,4096]{0,1:T(8,128)(2,1)}, f32[4096]{0:T(1024)S(1)}, f32[7,4096]{1,0:T(8,128)}, f32[256,64,128]{2,1,0:T(8,128)}) conditional(s32[]{:T(128)} %convert_element_type.250, () %tuple.115, (s32[]{:T(128)}, s32[2,1]{0,1:T(1,128)S(1)}, s32[64,1]{0,1:T(1,128)S(1)}, f32[2,4]{1,0:T(2,128)S(1)}, s32[]{:T(128)}, ...), branch_computations={%region_39.40_spmd, %region_40.51_spmd} | conditional | flops 1245062016 | bytes 179372352 | solution.py:175
  495.4 14.4 %conditional.17 = (bf16[64,4096]{0,1:T(8,128)(2,1)}, f32[4096]{0:T(1024)S(1)}, f32[7,4096]{1,0:T(8,128)}, f32[256,64,128]{2,1,0:T(8,128)}) conditional(s32[]{:T(128)} %convert_element_type.252, () %tuple.117, (s32[]{:T(128)}, s32[2,1]{0,1:T(1,128)S(1)}, s32[64,1]{0,1:T(1,128)S(1)}, f32[2,4]{1,0:T(2,128)S(1)}, s32[]{:T(128)}, ...), branch_computations={%region_51.52_spmd, %region_52.0_spmd} | conditional | flops 1245062016 | bytes 179437920 | solution.py:175
  515.4 314.0 %collective-permute-done.10 = bf16[64,4096]{1,0:T(8,128)(2,1)} collective-permute-done((bf16[64,4096]{1,0:T(8,128)(2,1)}, bf16[64,4096]{1,0:T(8,128)(2,1)}, u32[]{:S(2)}, u32[]{:S(2)}) %collective-permute-start.10) | collective-permute-done | bytes 524320 | tf_op jit(solution)/shard_map/ppermute | solution.py:17
  831.5 108.2 %conditional.18 = (bf16[64,4096]{0,1:T(8,128)(2,1)}, f32[4096]{0:T(1024)S(1)}, f32[7,4096]{1,0:T(8,128)}, f32[256,64,128]{2,1,0:T(8,128)}) conditional(s32[]{:T(128)} %convert_element_type.254, () %tuple.119, (s32[]{:T(128)}, s32[2,1]{0,1:T(1,128)S(1)}, s32[64,1]{0,1:T(1,128)S(1)}, f32[2,4]{1,0:T(2,128)S(1)}, s32[]{:T(128)}, ...), branch_computations={%region_63.64_spmd, %region_64.0_spmd} | conditional | flops 1245062016 | bytes 179372352 | solution.py:175
  858.0 16.7 %fusion.183 = f32[256,16,64]{2,1,0:T(8,128)} fusion(f32[128,256,16]{0,2,1:T(8,128)} %bitcast.565, f32[256,64,128]{2,1,0:T(8,128)} %copy.185), kind=kOutput, calls=%fused_computation.528 | convolution fusion | flops 402653184 | bytes 11534336 | tf_op jit(solution)/shard_map/cond/branch_1_fun/jvp(gts,sgk->tgk)/dot_general | solution.py:50
  922.6 16.9 %fusion.184 = f32[256,64,128]{2,1,0:T(8,128)} fusion(f32[256,16,64]{2,1,0:T(8,128)} %bitcast.560, f32[128,256,16]{0,2,1:T(8,128)} %bitcast.566), kind=kOutput, calls=%fused_computation.529 | convolution fusion | flops 402653184 | bytes 11534336 | tf_op jit(solution)/shard_map/cond/branch_1_fun/transpose(jvp(gts,sgk->tgk))/dot_general | solution.py:50
  965.9 101.2 %conditional.19 = (f32[4096]{0:T(1024)S(1)}, f32[7,4096]{1,0:T(8,128)S(1)}, f32[256,64,128]{2,1,0:T(8,128)}) conditional(s32[]{:T(128)} %convert_element_type.256, () %tuple.121, (s32[]{:T(128)}, bf16[2,64,4096]{2,1,0:T(8,128)(2,1)S(1)}, bf16[2,64,4096]{2,1,0:T(8,128)(2,1)}, s32[2,1]{0,1:T(1,128)}, s32[64,1]{0,1:T(1,128)}, ...), branch_computations={%region_75.76_spmd, %region_76.86_spmd} | conditional | flops 1244012800 | bytes 146779168 | solution.py:175
  994.8 16.7 %fusion.175 = f32[256,16,64]{2,1,0:T(8,128)} fusion(f32[128,256,16]{0,2,1:T(8,128)} %bitcast.569, f32[256,64,128]{2,1,0:T(8,128)} %copy.190), kind=kOutput, calls=%fused_computation.520 | convolution fusion | flops 402653184 | bytes 11534336 | tf_op jit(solution)/shard_map/cond/branch_1_fun/jvp(gts,sgk->tgk)/dot_general | solution.py:50
  1049.9 16.8 %fusion.176 = f32[256,64,128]{2,1,0:T(8,128)} fusion(f32[256,16,64]{2,1,0:T(8,128)} %bitcast.572, f32[128,256,16]{0,2,1:T(8,128)S(1)} %bitcast.570), kind=kOutput, calls=%fused_computation.521 | convolution fusion | flops 402653184 | bytes 11534336 | tf_op jit(solution)/shard_map/cond/branch_1_fun/transpose(jvp(gts,sgk->tgk))/dot_general | solution.py:50
  1069.1 19.8 %add_add_fusion.4 = f32[256,64,128]{2,1,0:T(8,128)} fusion(f32[256,64,128]{2,1,0:T(8,128)} %get-tuple-element.908, f32[256,64,128]{2,1,0:T(8,128)} %get-tuple-element.907, f32[256,64,128]{2,1,0:T(8,128)} %get-tuple-element.906, f32[256,64,128]{2,1,0:T(8,128)} %get-tuple-element.904, f32[256,64,128]{2,1,0:T(8,128)} %get-tuple-element.905), kind=kLoop, calls=%fused_computation.412 | loop fusion | flops 8388608 | bytes 50331648 | tf_op jit(solution)/shard_map/add | solution.py:176
  1088.9 13.8 %fusion.133 = f32[1,128,256]{2,1,0:T(8,128)} fusion(f32[256,64,128]{2,1,0:T(8,128)} %add_add_fusion.4, s32[64,128]{1,0:T(8,128)S(1)} %copy-done.90), kind=kOutput, calls=%fused_computation.418 | convolution fusion | flops 3222274048 | bytes 8552448 | tf_op jit(solution)/shard_map/tsj,gts->jg/dot_general | solution.py:36
  1104.0 16.7 %psum.21 = f32[1,4096]{1,0:T(1,128)} all-reduce(f32[1,4096]{1,0:T(1,128)S(1)} %bitcast.728), channel_id=1, replica_groups=mesh['groups'=2,'resp'=4,'section'=4] {'resp'}, use_global_device_ids=true, to_apply=%region_86.87 | all-reduce | flops 4096 | bytes 32768 | tf_op jit(solution)/shard_map/psum | solution.py:183
  1120.8 14.6 %all-reduce.92.cloned.1.call-done = (f32[1,7,4096]{2,0,1:T(1,128)}, f32[1,128,256]{2,1,0:T(8,128)}) async-done(((f32[1,7,4096]{2,0,1:T(1,128)}, f32[1,128,256]{2,1,0:T(8,128)}), (f32[1,7,4096]{2,0,1:T(1,128)}, f32[1,128,256]{2,1,0:T(8,128)})) %all-reduce.92.cloned.1.call-update) | async-done | bytes 245776 | tf_op jit(solution)/shard_map/psum | solution.py:183
  (379 shorter events, 363.5 us)
Async XLA Ops:
  7.2 56.0 %all-gather.20.cloned.1.call-start = ((), (), s32[]{:S(2)}) async-start(), calls=%async_computation.4 | async-start | bytes 2621440 | tf_op jit(solution)/shard_map/all_gather | solution.py:6
  14.5 103.3 %all-gather.18.cloned.1.call-start = ((), (), s32[]{:S(2)}) async-start(), calls=%async_computation.3 | async-start | bytes 2621440 | tf_op jit(solution)/shard_map/all_gather | solution.py:6
  15.3 140.6 %all-gather.16.cloned.1.call-start = ((), (), s32[]{:S(2)}) async-start(), calls=%async_computation.2 | async-start | bytes 2621440 | tf_op jit(solution)/shard_map/all_gather | solution.py:6
  16.0 185.9 %all-gather.14.cloned.1.call-start = ((), (), s32[]{:S(2)}) async-start(), calls=%async_computation.1 | async-start | bytes 2621440 | tf_op jit(solution)/shard_map/all_gather | solution.py:6
  16.6 231.5 %all-gather.12.cloned.1.call-start = ((), (), s32[]{:S(2)}) async-start(), calls=%async_computation | async-start | bytes 2621440 | tf_op jit(solution)/shard_map/all_gather | solution.py:6
  17.2 1118.2 %all-reduce.92.cloned.1.call-start = ((), (), s32[]{:S(2)}) async-start(), calls=%async_computation.5 | async-start | bytes 491520 | tf_op jit(solution)/shard_map/psum | solution.py:183
  111.9 140.2 %collective-permute-start = (bf16[64,4096]{1,0:T(8,128)(2,1)}, bf16[64,4096]{1,0:T(8,128)(2,1)}, u32[]{:S(2)}, u32[]{:S(2)}) collective-permute-start(bf16[64,4096]{1,0:T(8,128)(2,1)} %copy.151), channel_id=1, source_target_pairs={{0,1},{1,2},{2,3},{4,5},{5,6},{6,7},{8,9},{9,10},{10,11},{12,13},{... | collective-permute-start | bytes 1572872 | tf_op jit(solution)/shard_map/ppermute | solution.py:17
  298.4 5.2 collective-permute-start.1
  307.4 51.4 %collective-permute-start.2 = (bf16[64,4096]{1,0:T(8,128)(2,1)}, bf16[64,4096]{1,0:T(8,128)(2,1)}, u32[]{:S(2)}, u32[]{:S(2)}) collective-permute-start(bf16[64,4096]{1,0:T(8,128)(2,1)} %copy.159), channel_id=1, source_target_pairs={{0,1},{1,2},{2,3},{4,5},{5,6},{6,7},{8,9},{9,10},{10,11},{12,13},{... | collective-permute-start | bytes 1572872 | tf_op jit(solution)/shard_map/ppermute | solution.py:17
  362.5 10.9 collective-permute-start.3
  408.2 54.8 %copy-start.104 = (f32[4096]{0:T(1024)}, f32[4096]{0:T(1024)S(1)}, u32[]{:S(2)}) copy-start(f32[4096]{0:T(1024)S(1)} %get-tuple-element.890) | copy-start | bytes 49156
  408.2 54.8 %copy-start.138 = (f32[64,1]{0,1:T(1,128)S(1)}, f32[64,1]{0,1:T(1,128)}, u32[]{:S(2)}) copy-start(f32[64,1]{0,1:T(1,128)} %copy-done.137) | copy-start | bytes 772
  410.6 50.3 %collective-permute-start.8 = (bf16[64,4096]{1,0:T(8,128)(2,1)}, bf16[64,4096]{1,0:T(8,128)(2,1)}, u32[]{:S(2)}, u32[]{:S(2)}) collective-permute-start(bf16[64,4096]{1,0:T(8,128)(2,1)} %copy.171), channel_id=1, source_target_pairs={{1,0},{2,1},{3,2},{5,4},{6,5},{7,6},{9,8},{10,9},{11,10},{13,12},{... | collective-permute-start | bytes 1572872 | tf_op jit(solution)/shard_map/ppermute | solution.py:17
  479.7 13.6 %collective-permute-start.9 = (bf16[64,4096]{1,0:T(8,128)(2,1)}, bf16[64,4096]{1,0:T(8,128)(2,1)}, u32[]{:S(2)}, u32[]{:S(2)}) collective-permute-start(bf16[64,4096]{1,0:T(8,128)(2,1)} %copy.176), channel_id=1, source_target_pairs={{1,0},{2,1},{3,2},{5,4},{6,5},{7,6},{9,8},{10,9},{11,10},{13,12},{... | collective-permute-start | bytes 1572872 | tf_op jit(solution)/shard_map/ppermute | solution.py:17
  509.8 321.6 %copy-start.108 = (f32[4096]{0:T(1024)}, f32[4096]{0:T(1024)S(1)}, u32[]{:S(2)}) copy-start(f32[4096]{0:T(1024)S(1)} %get-tuple-element.894) | copy-start | bytes 49156
  509.8 321.6 %copy-start.140 = (f32[64,1]{0,1:T(1,128)S(1)}, f32[64,1]{0,1:T(1,128)}, u32[]{:S(2)}) copy-start(f32[64,1]{0,1:T(1,128)} %copy-done.137) | copy-start | bytes 772
  509.8 321.6 %copy-start.145 = (s32[2,1]{0,1:T(1,128)S(1)}, s32[2,1]{0,1:T(1,128)}, u32[]{:S(2)}) copy-start(s32[2,1]{0,1:T(1,128)} %param.35) | copy-start | bytes 28
  509.9 321.6 %copy-start.150 = (f32[2,4]{1,0:T(2,128)S(1)}, f32[2,4]{1,0:T(2,128)}, u32[]{:S(2)}) copy-start(f32[2,4]{1,0:T(2,128)} %copy-done.147) | copy-start | bytes 100
  512.2 317.1 %collective-permute-start.10 = (bf16[64,4096]{1,0:T(8,128)(2,1)}, bf16[64,4096]{1,0:T(8,128)(2,1)}, u32[]{:S(2)}, u32[]{:S(2)}) collective-permute-start(bf16[64,4096]{1,0:T(8,128)(2,1)} %copy.181), channel_id=1, source_target_pairs={{1,0},{2,1},{3,2},{5,4},{6,5},{7,6},{9,8},{10,9},{11,10},{13,12},{... | collective-permute-start | bytes 1572872 | tf_op jit(solution)/shard_map/ppermute | solution.py:17
  514.1 429.3 %collective-permute-start.4 = (bf16[2]{0:T(256)(128)(2,1)}, bf16[2]{0:T(256)(128)(2,1)}, u32[]{:S(2)}, u32[]{:S(2)}) collective-permute-start(bf16[2]{0:T(256)(128)(2,1)} %fusion.156), channel_id=1, source_target_pairs={{1,0},{2,1},{3,2},{5,4},{6,5},{7,6},{9,8},{10,9},{11,10},{13,12},{... | collective-permute-start | bytes 20 | tf_op jit(solution)/shard_map/ppermute | solution.py:17
  942.1 22.3 %collective-permute-start.11 = (bf16[64,4096]{1,0:T(8,128)(2,1)}, bf16[64,4096]{1,0:T(8,128)(2,1)S(1)}, u32[]{:S(2)}, u32[]{:S(2)}) collective-permute-start(bf16[64,4096]{1,0:T(8,128)(2,1)} %copy.186), channel_id=1, source_target_pairs={{1,0},{2,1},{3,2},{5,4},{6,5},{7,6},{9,8},{10,9},{11,10},{13,12},{... | collective-permute-start | bytes 1572872 | tf_op jit(solution)/shard_map/ppermute | solution.py:17
  944.1 10.3 collective-permute-start.5
  954.4 8.1 collective-permute-start.6
  963.1 139.7 %collective-permute-start.7 = (bf16[2]{0:T(256)(128)(2,1)}, bf16[2]{0:T(256)(128)(2,1)}, u32[]{:S(2)}, u32[]{:S(2)}) collective-permute-start(bf16[2]{0:T(256)(128)(2,1)} %broadcast_select_fusion.6), channel_id=1, source_target_pairs={{1,0},{2,1},{3,2},{5,4},{6,5},{7,6},{9,8},{10,9},{11,10},{13,12},{... | collective-permute-start | bytes 20 | tf_op jit(solution)/shard_map/ppermute | solution.py:17
  (86 other events, 1086.6 us)
Sparse Core Ops, SparseCore 0:
  14.7 48.4 all-gather.19
  64.8 44.8 all-gather.17
  111.2 44.6 all-gather.15
  157.3 44.6 all-gather.13
  203.4 44.6 all-gather.11
  1102.9 32.4 all-reduce.91
